TPU v7x, 128 devices: a whole 4x4x4 slice. The times are simulated.
128 devices in a mesh: dense: 32 (over x, z, core), attn: 4 (over y).
Axes of the slice: x: 4, y: 4, z: 4, core: 2. Of those that a mesh axis runs over, the one named last changes fastest.
Arguments:
- queries: bfloat16 [8192, 4096], P('dense', 'attn'), may hold values from -30 to 30
- keys: bfloat16 [8192, 1024], P('dense', 'attn'), may hold values from -13 to 13
- values: bfloat16 [8192, 1024], P('dense', 'attn'), may hold values from -24 to 24
- segments: int32 [8192], replicated, may hold values from 0 to 5, never falling along the last dimension, each value on 1 to 4096 neighbouring positions
- out_weight: bfloat16 [4096, 4096], P('attn', 'dense'), may hold values from -0.09375 to 0.09375
Outputs:
- projected: bfloat16 [8192, 4096], P('dense', 'attn')
All inputs are finite; a program needn't handle non-finite values.
Results may differ from a plain program's by a relative error of at most 0.012.
Values may be sent and summed in bfloat16 or wider, within the bound.
A program may use at most 128 MiB of HBM per device.

v0:
```python
import math
import jax
import jax.numpy as jnp
from jax import lax
from jax.sharding import PartitionSpec as P

HEAD_WIDTH = 128
NEGATIVE = -1e30


def attend(query_rows, positions, query_docs, keys, values, segments):
    token_count = query_rows.shape[0]
    kv_local = keys.shape[1] // HEAD_WIDTH
    head_group = query_rows.shape[1] // HEAD_WIDTH // kv_local
    blocks_count = max(token_count // 128, 1)
    block_rows = token_count // blocks_count
    inv_root = 1.0 / math.sqrt(HEAD_WIDTH)
    query_heads = query_rows.reshape(token_count, kv_local, head_group, HEAD_WIDTH)
    initial = tuple(
        (
            (
                jnp.full((kv_local, head_group, block_rows), NEGATIVE, jnp.float32),
                jnp.zeros((kv_local, head_group, block_rows), jnp.float32),
                jnp.zeros((kv_local, head_group, block_rows, HEAD_WIDTH), jnp.float32),
            )
            for which_block in range(blocks_count)
        )
    )
    key_piece = lax.all_gather(keys, "dense", axis=0, tiled=True)
    value_piece = lax.all_gather(values, "dense", axis=0, tiled=True)
    key_count = key_piece.shape[0]
    key_positions = jnp.arange(key_count, dtype=jnp.int32)
    key_heads = key_piece.reshape(key_count, kv_local, HEAD_WIDTH)
    value_heads = value_piece.reshape(key_count, kv_local, HEAD_WIDTH)
    updated = []
    for which_block in range(blocks_count):
        lower = which_block * block_rows
        upper = lower + block_rows
        visible = (query_docs[lower:upper, None] == segments[None, :]) & (
            key_positions[None, :] <= positions[lower:upper, None]
        )
        sliced = query_heads[lower:upper]

        def compute(state):
            row_max, totals, summed = state
            scores = (
                jnp.einsum("qgjd,kgd->gjqk", sliced, key_heads, preferred_element_type=jnp.float32)
                * inv_root
            )
            scores = jnp.where(visible, scores, NEGATIVE)
            new_max = jnp.maximum(row_max, jnp.max(scores, axis=-1))
            weights = jnp.where(visible, jnp.exp(scores - new_max[..., None]), 0.0)
            totals = jnp.sum(weights, axis=-1)
            summed = jnp.einsum(
                "gjqk,kgd->gjqd",
                weights.astype(jnp.bfloat16),
                value_heads,
                preferred_element_type=jnp.float32,
            )
            return (new_max, totals, summed)

        updated.append(
            lax.cond(jnp.any(visible), compute, lambda state: state, initial[which_block])
        )
    final = tuple(updated)
    outputs = []
    for state in final:
        outputs.append(state[2] / state[1][..., None])
    attended = jnp.concatenate(outputs, axis=2).astype(jnp.bfloat16)
    return attended.transpose(2, 0, 1, 3).reshape(token_count, kv_local * head_group * HEAD_WIDTH)


def project(attended, out_weight):
    partial_sums = jnp.dot(
        attended,
        lax.all_gather(out_weight, "dense", axis=1, tiled=True),
        preferred_element_type=jnp.float32,
    )
    return lax.psum_scatter(
        partial_sums.astype(jnp.bfloat16), "attn", scatter_dimension=1, tiled=True
    )


def shards(queries, keys, values, segments, out_weight):
    device_index = lax.axis_index("dense")
    token_count = queries.shape[0]
    positions = device_index * token_count + jnp.arange(token_count, dtype=jnp.int32)
    query_docs = lax.dynamic_slice_in_dim(segments, device_index * token_count, token_count)
    attended = attend(queries, positions, query_docs, keys, values, segments)
    projected = project(attended, out_weight)
    return projected


def solution(mesh):
    return jax.shard_map(
        shards,
        mesh=mesh,
        in_specs=(
            P("dense", "attn"),
            P("dense", "attn"),
            P("dense", "attn"),
            P(),
            P("attn", "dense"),
        ),
        out_specs=P("dense", "attn"),
        check_vma=False,
    )
```

profile of v0, /device:TPU:1, one launch (start us, length us, event | category | flops | bytes accessed | tf_op | source)
XLA Modules:
  0.0 251.5 jit_solution(4987157832332547177)
XLA Ops:
  6.5 1.7 copy.12
  8.2 0.0 all-gather.6.cloned.1.call-start
  8.3 1.6 copy.13
  9.9 0.0 all-gather.8.cloned.1.call-start
  10.0 0.7 all-gather.8.cloned.1.call-update
  10.7 0.8 dynamic_slice.3
  11.5 4.9 %fusion.27 = (pred[]{:T(512)}, pred[]{:T(512)}, pred[128,8192]{0,1:T(8,128)(4,1)S(1)}, pred[128,8192]{0,1:T(8,128)(4,1)S(1)}) fusion(s32[128]{0:T(128)S(1)} %get-tuple-element.63, s32[8192]{0:T(1024)} %param.12, s32[128]{0:T(128)S(1)} %get-tuple-element.60, s32[128]{0:T(128)S(1)} %get-tuple-element.64, s32[128]{0:T(128)S(1)} %get-tuple-element.59), kind=kLoop, calls=%fused_computation.38 | loop fusion | flops 8388606 | bytes 2131970 | tf_op jit(solution)/shard_map/reduce_or | solution.py:63
  17.6 44.3 %all-gather.4.cloned.1.call-done = bf16[8192,256]{0,1:T(8,128)(2,1)} async-done(((bf16[256,256]{0,1:T(8,128)(2,1)}), bf16[8192,256]{0,1:T(8,128)(2,1)}) %all-gather.4.cloned.1.call-update) | async-done | bytes 4194320 | tf_op jit(solution)/shard_map/all_gather | solution.py:29
  61.9 50.4 %all-gather.6.cloned.1.call-done = bf16[8192,256]{0,1:T(8,128)(2,1)} async-done(((bf16[256,256]{0,1:T(8,128)(2,1)}), bf16[8192,256]{0,1:T(8,128)(2,1)}) %all-gather.6.cloned.1.call-update) | async-done | bytes 4194320 | tf_op jit(solution)/shard_map/all_gather | solution.py:30
  112.2 48.2 %conditional.2 = (f32[2,4,128]{2,1,0:T(4,128)S(1)}, f32[2,4,128,128]{2,3,1,0:T(8,128)S(1)}) conditional(s32[]{:T(128)} %convert_element_type.16, () %tuple.21, (pred[128,8192]{0,1:T(8,128)(4,1)S(1)}, bf16[256,1024]{1,0:T(8,128)(2,1)}, bf16[8192,2,128]{0,2,1:T(8,128)(2,1)}, bf16[8192,2,128]{0,2,1:T(8,128)(2,1)}) %tuple.54), branch_computations={%region_1.0_spmd, %region_2.5_spmd} | conditional | flops 4404018176 | bytes 114581520 | solution.py:63
  112.2 1.2 copy.14
  113.5 16.2 %fusion = (f32[2,4,128]{2,1,0:T(4,128)S(1)}, f32[2,8192,128,4]{2,1,3,0:T(8,128)}) fusion(pred[128,8192]{0,1:T(8,128)(4,1)S(1)} %get-tuple-element.25, bf16[128,2,4,128]{0,3,2,1:T(8,128)(2,1)S(1)} %bitcast.60, bf16[8192,2,128]{0,2,1:T(8,128)(2,1)} %get-tuple-element.43), kind=kOutput, calls=%fused_computation.2 | convolution fusion | flops 2172648448 | bytes 39063552 | tf_op jit(solution)/shard_map/cond/branch_1_fun/qgjd,kgd->gjqk/dot_general | solution.py:47
  129.8 15.5 %fusion.3 = f32[2,4,128,128]{2,3,1,0:T(8,128)S(1)} fusion(f32[2,8192,128,4]{2,1,3,0:T(8,128)} %get-tuple-element.54, f32[2,4,128]{2,1,0:T(4,128)S(1)} %broadcast_maximum_fusion, pred[128,8192]{0,1:T(8,128)(4,1)S(1)} %get-tuple-element.25, bf16[8192,2,128]{0,2,1:T(8,128)(2,1)} %get-tuple-element.44), kind=kOutput, calls=%fused_computation.5 | convolution fusion | flops 2189426688 | bytes 39325696 | tf_op jit(solution)/shard_map/cond | solution.py:63
  145.2 15.2 %fusion.2 = f32[2,4,128]{2,1,0:T(4,128)S(1)} fusion(f32[2,8192,128,4]{2,1,3,0:T(8,128)} %get-tuple-element.54, f32[2,4,128]{2,1,0:T(4,128)S(1)} %broadcast_maximum_fusion, pred[128,8192]{0,1:T(8,128)(4,1)S(1)} %get-tuple-element.25), kind=kLoop, calls=%fused_computation.4 | loop fusion | flops 41942016 | bytes 34611200 | tf_op jit(solution)/shard_map/cond/branch_1_fun/reduce_sum | solution.py:53
  160.4 47.9 %conditional.3 = (f32[2,4,128]{2,1,0:T(4,128)S(1)}, f32[2,4,128,128]{2,3,1,0:T(8,128)S(1)}) conditional(s32[]{:T(128)} %convert_element_type.17, () %tuple.23, (pred[128,8192]{0,1:T(8,128)(4,1)S(1)}, bf16[256,1024]{1,0:T(8,128)(2,1)}, bf16[8192,2,128]{0,2,1:T(8,128)(2,1)}, bf16[8192,2,128]{0,2,1:T(8,128)(2,1)}) %tuple.55), branch_computations={%region_6.7_spmd, %region_7.10_spmd} | conditional | flops 4404018176 | bytes 114581520 | solution.py:63
  160.6 1.2 copy.18
  161.9 16.3 %fusion.12 = (f32[2,4,128]{2,1,0:T(4,128)S(1)}, f32[2,8192,128,4]{2,1,3,0:T(8,128)}) fusion(pred[128,8192]{0,1:T(8,128)(4,1)S(1)} %get-tuple-element.29, bf16[128,2,4,128]{0,3,2,1:T(8,128)(2,1)S(1)} %bitcast.61, bf16[8192,2,128]{0,2,1:T(8,128)(2,1)} %get-tuple-element.47), kind=kOutput, calls=%fused_computation.16 | convolution fusion | flops 2172648448 | bytes 39063552 | tf_op jit(solution)/shard_map/cond/branch_1_fun/qgjd,kgd->gjqk/dot_general | solution.py:47
  178.3 15.4 %fusion.15 = f32[2,4,128,128]{2,3,1,0:T(8,128)S(1)} fusion(f32[2,8192,128,4]{2,1,3,0:T(8,128)} %get-tuple-element.56, f32[2,4,128]{2,1,0:T(4,128)S(1)} %broadcast_maximum_fusion.1, pred[128,8192]{0,1:T(8,128)(4,1)S(1)} %get-tuple-element.29, bf16[8192,2,128]{0,2,1:T(8,128)(2,1)} %get-tuple-element.48), kind=kOutput, calls=%fused_computation.19 | convolution fusion | flops 2189426688 | bytes 39325696 | tf_op jit(solution)/shard_map/cond | solution.py:63
  193.7 14.7 %fusion.14 = f32[2,4,128]{2,1,0:T(4,128)S(1)} fusion(f32[2,8192,128,4]{2,1,3,0:T(8,128)} %get-tuple-element.56, f32[2,4,128]{2,1,0:T(4,128)S(1)} %broadcast_maximum_fusion.1, pred[128,8192]{0,1:T(8,128)(4,1)S(1)} %get-tuple-element.29), kind=kLoop, calls=%fused_computation.18 | loop fusion | flops 41942016 | bytes 34611200 | tf_op jit(solution)/shard_map/cond/branch_1_fun/reduce_sum | solution.py:53
  208.3 0.1 divide_convert_fusion.1
  208.4 0.1 divide_convert_fusion
  208.5 0.1 pad_maximum_fusion
  208.6 7.1 %convolution_convert_fusion = bf16[256,4096]{1,0:T(8,128)(2,1)} fusion(bf16[256,1024]{0,1:T(8,128)(2,1)S(1)} %bitcast.59, bf16[1024,4096]{1,0:T(8,128)(2,1)} %all-gather.8.cloned.1.call-done), kind=kOutput, calls=%fused_computation.28 | convolution fusion | flops 2148532224 | bytes 11010048 | tf_op jit(solution)/shard_map/dot_general | solution.py:74
  215.7 29.3 %reduce-scatter.2.cloned.1.call-done = bf16[256,1024]{1,0:T(8,128)(2,1)} async-done(((bf16[256,4096]{1,0:T(8,128)(2,1)}), bf16[256,1024]{1,0:T(8,128)(2,1)}) %reduce-scatter.2.cloned.1.call-update) | async-done | bytes 524304 | tf_op jit(solution)/shard_map/reduce_scatter | solution.py:79
  (12 shorter events, 0.2 us)
Async XLA Ops:
  6.5 55.3 %all-gather.4.cloned.1.call-start = ((), (), s32[]{:S(2)}) async-start(), calls=%async_computation.1 | async-start | bytes 4325376 | tf_op jit(solution)/shard_map/all_gather | solution.py:29
  8.2 104.0 %all-gather.6.cloned.1.call-start = ((), (), s32[]{:S(2)}) async-start(), calls=%async_computation.2 | async-start | bytes 4325376 | tf_op jit(solution)/shard_map/all_gather | solution.py:30
  9.9 198.6 %all-gather.8.cloned.1.call-start = ((), (), s32[]{:S(2)}) async-start(), calls=%async_computation.3 | async-start | bytes 8650752 | tf_op jit(solution)/shard_map/all_gather | solution.py:76
  10.7 234.3 %reduce-scatter.2.cloned.1.call-start = ((), (), s32[]{:S(2)}) async-start(), calls=%async_computation.4 | async-start | bytes 2621440 | tf_op jit(solution)/shard_map/reduce_scatter | solution.py:79
Sparse Core Ops, SparseCore 0:
  9.5 52.3 all-gather.3
  64.0 48.1 all-gather.5
  114.4 58.3 all-gather.7
  215.8 29.1 reduce-scatter.1
where the time goes:
time: 252 us
  waiting for transfers between devices  125 us (50%)
  matrix products  70.6 us (28%)
  other arithmetic  35 us (14%)
  between operations  14.3 us (6%)
  local copies, waits for them, and re-layouts  6.61 us (3%)
    all_gather x1, waiting for transfers between devices, attend(): value_piece = lax.all_gather(values, 'dense', axis=0, tiled=True)  50.4 us
    all_gather x1, waiting for transfers between devices, attend(): key_piece = lax.all_gather(keys, 'dense', axis=0, tiled=True)  44.3 us
    dot_general x2, matrix products, compute(): jnp.einsum('qgjd,kgd->gjqk', sliced, key_heads, preferred_element_type=jn...  32.6 us
    cond x2, matrix products, attend(): lax.cond(jnp.any(visible), compute, lambda state: state, initial[which_bl...  30.9 us
    reduce_sum x2, other arithmetic, compute(): totals = jnp.sum(weights, axis=-1)  29.9 us
    reduce_scatter x1, waiting for transfers between devices, project(): lax.psum_scatter(partial_sums.astype(jnp.bfloat16), 'attn', scatter_dimen...  29.3 us
    dot_general x1, matrix products, project(): jnp.dot(attended, lax.all_gather(out_weight, 'dense', axis=1, tiled=True)...  7.11 us
  transfers between devices with their start and end apart: 4, of which 3 were waited for; matrix products, arithmetic and copies ran while one was open for 41% of the time, Pallas kernels for 0%

commit v1 on v0

--- a/solution.py
+++ b/solution.py
@@ -27,7 +27,10 @@
         )
     )
     key_piece = lax.all_gather(keys, "dense", axis=0, tiled=True)
-    value_piece = lax.all_gather(values, "dense", axis=0, tiled=True)
+    n_dev = lax.axis_size("dense")
+    shards_2 = jnp.stack([values for _ in range(n_dev)])
+    shards_2 = lax.all_to_all(shards_2, "dense", split_axis=0, concat_axis=0)
+    value_piece = jnp.concatenate(shards_2, axis=0)
     key_count = key_piece.shape[0]
     key_positions = jnp.arange(key_count, dtype=jnp.int32)
     key_heads = key_piece.reshape(key_count, kv_local, HEAD_WIDTH)

time: 252 us -> 234 us (0.929)
  waiting for transfers between devices: 125 us -> 80.6 us
  local copies, waits for them, and re-layouts: 6.61 us -> 22.4 us
  starting transfers between devices: 0.12 us -> 9.56 us
    all_gather x1 -> x0, waiting for transfers between devices: 50.4 us -> none  [attend(): value_piece = lax.all_gather(values, 'dense', axis=0, tiled=True)]
    all_to_all x0 -> x1, waiting for transfers between devices: none -> 47.2 us  [attend(): shards_2 = lax.all_to_all(shards_2, 'dense', split_axis=0, concat_axis=0)]
    all_gather x1, waiting for transfers between devices: 44.3 us -> 1.06 us  [attend(): key_piece = lax.all_gather(keys, 'dense', axis=0, tiled=True)]
    another operation x2 -> x4, local copies, waits for them, and re-layouts: 2.49 us -> 12.4 us  [the longest x1 7.47 us: attend(): value_heads = value_piece.reshape(key_count, kv_local, HEAD_WIDTH)]
    all_to_all x0 -> x1, starting transfers between devices: none -> 9.47 us  [attend(): shards_2 = lax.all_to_all(shards_2, 'dense', split_axis=0, concat_axis=0)]
    all_to_all x0 -> x1, local copies, waits for them, and re-layouts: none -> 6.53 us  [attend(): shards_2 = lax.all_to_all(shards_2, 'dense', split_axis=0, concat_axis=0)]
  transfers between devices with their start and end apart: 4 -> 4, of which waited for: 3 -> 3; matrix products, arithmetic and copies ran while one was open for 41% -> 51% of each run, Pallas kernels for 0% -> 0%
where the time goes in v1:
time: 234 us; the launch traced here: 233 us
  waiting for transfers between devices  80.6 us (34%)
  matrix products  70.4 us (30%)
  other arithmetic  35.3 us (15%)
  local copies, waits for them, and re-layouts  22.4 us (10%)
  between operations  14.4 us (6%)
  starting transfers between devices  9.56 us (4%)
    all_to_all x1, waiting for transfers between devices, attend(): shards_2 = lax.all_to_all(shards_2, 'dense', split_axis=0, concat_axis=0)  47.2 us
    dot_general x2, matrix products, compute(): jnp.einsum('qgjd,kgd->gjqk', sliced, key_heads, preferred_element_type=jn...  32.4 us
    reduce_scatter x1, waiting for transfers between devices, project(): lax.psum_scatter(partial_sums.astype(jnp.bfloat16), 'attn', scatter_dimen...  31.6 us
    cond x2, matrix products, attend(): lax.cond(jnp.any(visible), compute, lambda state: state, initial[which_bl...  30.9 us
    reduce_sum x2, other arithmetic, compute(): totals = jnp.sum(weights, axis=-1)  30.1 us
    all_to_all x1, starting transfers between devices, attend(): shards_2 = lax.all_to_all(shards_2, 'dense', split_axis=0, concat_axis=0)  9.47 us
    another operation x1, local copies, waits for them, and re-layouts, attend(): value_heads = value_piece.reshape(key_count, kv_local, HEAD_WIDTH)  7.47 us
    dot_general x1, matrix products, project(): jnp.dot(attended, lax.all_gather(out_weight, 'dense', axis=1, tiled=True)...  7.11 us
  transfers between devices with their start and end apart: 4, of which 3 were waited for; matrix products, arithmetic and copies ran while one was open for 51% of the time, Pallas kernels for 0%

profile of v1, /device:TPU:1, one launch (start us, length us, event | category | flops | bytes accessed | tf_op | source)
XLA Modules:
  0.0 233.0 jit_solution(6694397534285832988)
XLA Ops:
  6.5 1.7 copy.26
  8.3 0.7 all-gather.5.cloned.1.call-update
  9.0 1.0 copy.27
  10.0 2.4 %stack.2 = bf16[32,256,256]{1,2,0:T(8,128)(2,1)} broadcast(bf16[256,256]{0,1:T(8,128)(2,1)S(1)} %copy.27), dimensions={1,2} | broadcast | bytes 4325376 | tf_op jit(solution)/shard_map/stack | solution.py:31
  12.4 9.5 %all-to-all-start = ((bf16[32,256,256]{1,2,0:T(8,128)(2,1)}), bf16[32,256,256]{1,2,0:T(8,128)(2,1)}, u32[]{:S(2)}, u32[]{:S(2)}) async-start(bf16[32,256,256]{1,2,0:T(8,128)(2,1)} %stack.2), calls=%async_computation | async-start | bytes 8388608 | tf_op jit(solution)/shard_map/all_to_all | solution.py:32
  22.0 0.8 dynamic_slice.3
  22.7 4.9 %fusion.27 = (pred[]{:T(512)}, pred[]{:T(512)}, pred[128,8192]{0,1:T(8,128)(4,1)S(1)}, pred[128,8192]{0,1:T(8,128)(4,1)S(1)}) fusion(s32[128]{0:T(128)S(1)} %get-tuple-element.71, s32[8192]{0:T(1024)} %param.12, s32[128]{0:T(128)S(1)} %get-tuple-element.68, s32[128]{0:T(128)S(1)} %get-tuple-element.72, s32[128]{0:T(128)S(1)} %get-tuple-element.67), kind=kLoop, calls=%fused_computation.38 | loop fusion | flops 8388606 | bytes 2131970 | tf_op jit(solution)/shard_map/reduce_or | solution.py:66
  29.0 47.2 %all-to-all-done = bf16[32,256,256]{1,2,0:T(8,128)(2,1)} async-done(((bf16[32,256,256]{1,2,0:T(8,128)(2,1)}), bf16[32,256,256]{1,2,0:T(8,128)(2,1)}, u32[]{:S(2)}, u32[]{:S(2)}) %all-to-all-start) | async-done | bytes 4194336 | tf_op jit(solution)/shard_map/all_to_all | solution.py:32
  76.1 6.5 %copy.28 = bf16[32,256,256]{1,0,2:T(8,128)(2,1)} copy(bf16[32,256,256]{1,2,0:T(8,128)(2,1)} %all-to-all-done) | data formatting | bytes 8388608 | tf_op jit(solution)/shard_map/all_to_all | solution.py:32
  82.7 7.5 %reshape_reshape.3 = bf16[8192,2,128]{0,2,1:T(8,128)(2,1)} reshape(bf16[32,256,256]{1,0,2:T(8,128)(2,1)} %copy.28) | data formatting | bytes 8388608 | tf_op jit(solution)/shard_map/reshape;reshape | solution.py:37
  90.1 1.1 all-gather.3.cloned.1.call-done
  91.2 48.5 %conditional.2 = (f32[2,4,128]{2,1,0:T(4,128)S(1)}, f32[2,4,128,128]{2,3,1,0:T(8,128)S(1)}) conditional(s32[]{:T(128)} %convert_element_type.16, () %tuple.21, (pred[128,8192]{0,1:T(8,128)(4,1)S(1)}, bf16[256,1024]{1,0:T(8,128)(2,1)}, bf16[8192,2,128]{0,2,1:T(8,128)(2,1)}, bf16[8192,2,128]{0,2,1:T(8,128)(2,1)}) %tuple.52), branch_computations={%region_1.0_spmd, %region_2.5_spmd} | conditional | flops 4404018176 | bytes 114581520 | solution.py:66
  91.2 1.2 copy.29
  92.5 16.2 %fusion = (f32[2,4,128]{2,1,0:T(4,128)S(1)}, f32[2,8192,128,4]{2,1,3,0:T(8,128)}) fusion(pred[128,8192]{0,1:T(8,128)(4,1)S(1)} %get-tuple-element.25, bf16[128,2,4,128]{0,3,2,1:T(8,128)(2,1)S(1)} %bitcast.61, bf16[8192,2,128]{0,2,1:T(8,128)(2,1)} %get-tuple-element.51), kind=kOutput, calls=%fused_computation.2 | convolution fusion | flops 2172648448 | bytes 39063552 | tf_op jit(solution)/shard_map/cond/branch_1_fun/qgjd,kgd->gjqk/dot_general | solution.py:50
  108.7 15.5 %fusion.3 = f32[2,4,128,128]{2,3,1,0:T(8,128)S(1)} fusion(f32[2,8192,128,4]{2,1,3,0:T(8,128)} %get-tuple-element.62, f32[2,4,128]{2,1,0:T(4,128)S(1)} %broadcast_maximum_fusion, pred[128,8192]{0,1:T(8,128)(4,1)S(1)} %get-tuple-element.25, bf16[8192,2,128]{0,2,1:T(8,128)(2,1)} %get-tuple-element.52), kind=kOutput, calls=%fused_computation.5 | convolution fusion | flops 2189426688 | bytes 39325696 | tf_op jit(solution)/shard_map/cond | solution.py:66
  124.2 15.4 %fusion.2 = f32[2,4,128]{2,1,0:T(4,128)S(1)} fusion(f32[2,8192,128,4]{2,1,3,0:T(8,128)} %get-tuple-element.62, f32[2,4,128]{2,1,0:T(4,128)S(1)} %broadcast_maximum_fusion, pred[128,8192]{0,1:T(8,128)(4,1)S(1)} %get-tuple-element.25), kind=kLoop, calls=%fused_computation.4 | loop fusion | flops 41942016 | bytes 34611200 | tf_op jit(solution)/shard_map/cond/branch_1_fun/reduce_sum | solution.py:56
  139.6 47.8 %conditional.3 = (f32[2,4,128]{2,1,0:T(4,128)S(1)}, f32[2,4,128,128]{2,3,1,0:T(8,128)S(1)}) conditional(s32[]{:T(128)} %convert_element_type.17, () %tuple.23, (pred[128,8192]{0,1:T(8,128)(4,1)S(1)}, bf16[256,1024]{1,0:T(8,128)(2,1)}, bf16[8192,2,128]{0,2,1:T(8,128)(2,1)}, bf16[8192,2,128]{0,2,1:T(8,128)(2,1)}) %tuple.53), branch_computations={%region_6.7_spmd, %region_7.10_spmd} | conditional | flops 4404018176 | bytes 114581520 | solution.py:66
  139.9 1.2 copy.33
  141.2 16.2 %fusion.12 = (f32[2,4,128]{2,1,0:T(4,128)S(1)}, f32[2,8192,128,4]{2,1,3,0:T(8,128)}) fusion(pred[128,8192]{0,1:T(8,128)(4,1)S(1)} %get-tuple-element.29, bf16[128,2,4,128]{0,3,2,1:T(8,128)(2,1)S(1)} %bitcast.62, bf16[8192,2,128]{0,2,1:T(8,128)(2,1)} %get-tuple-element.55), kind=kOutput, calls=%fused_computation.16 | convolution fusion | flops 2172648448 | bytes 39063552 | tf_op jit(solution)/shard_map/cond/branch_1_fun/qgjd,kgd->gjqk/dot_general | solution.py:50
  157.4 15.4 %fusion.15 = f32[2,4,128,128]{2,3,1,0:T(8,128)S(1)} fusion(f32[2,8192,128,4]{2,1,3,0:T(8,128)} %get-tuple-element.64, f32[2,4,128]{2,1,0:T(4,128)S(1)} %broadcast_maximum_fusion.1, pred[128,8192]{0,1:T(8,128)(4,1)S(1)} %get-tuple-element.29, bf16[8192,2,128]{0,2,1:T(8,128)(2,1)} %get-tuple-element.56), kind=kOutput, calls=%fused_computation.19 | convolution fusion | flops 2189426688 | bytes 39325696 | tf_op jit(solution)/shard_map/cond | solution.py:66
  172.8 14.7 %fusion.14 = f32[2,4,128]{2,1,0:T(4,128)S(1)} fusion(f32[2,8192,128,4]{2,1,3,0:T(8,128)} %get-tuple-element.64, f32[2,4,128]{2,1,0:T(4,128)S(1)} %broadcast_maximum_fusion.1, pred[128,8192]{0,1:T(8,128)(4,1)S(1)} %get-tuple-element.29), kind=kLoop, calls=%fused_computation.18 | loop fusion | flops 41942016 | bytes 34611200 | tf_op jit(solution)/shard_map/cond/branch_1_fun/reduce_sum | solution.py:56
  187.6 0.1 pad_maximum_fusion
  187.7 7.1 %convolution_convert_fusion = bf16[256,4096]{1,0:T(8,128)(2,1)} fusion(bf16[256,1024]{0,1:T(8,128)(2,1)S(1)} %bitcast.60, bf16[1024,4096]{1,0:T(8,128)(2,1)} %all-gather.5.cloned.1.call-done), kind=kOutput, calls=%fused_computation.28 | convolution fusion | flops 2148532224 | bytes 11010048 | tf_op jit(solution)/shard_map/dot_general | solution.py:77
  194.8 31.6 %reduce-scatter.2.cloned.1.call-done = bf16[256,1024]{1,0:T(8,128)(2,1)} async-done(((bf16[256,4096]{1,0:T(8,128)(2,1)}), bf16[256,1024]{1,0:T(8,128)(2,1)}) %reduce-scatter.2.cloned.1.call-update) | async-done | bytes 524304 | tf_op jit(solution)/shard_map/reduce_scatter | solution.py:82
  (14 shorter events, 0.3 us)
Async XLA Ops:
  6.5 84.6 %all-gather.3.cloned.1.call-start = ((), (), s32[]{:S(2)}) async-start(), calls=%async_computation.2 | async-start | bytes 4325376 | tf_op jit(solution)/shard_map/all_gather | solution.py:29
  8.2 179.5 %all-gather.5.cloned.1.call-start = ((), (), s32[]{:S(2)}) async-start(), calls=%async_computation.3 | async-start | bytes 8650752 | tf_op jit(solution)/shard_map/all_gather | solution.py:79
  12.4 63.7 %all-to-all-start = ((bf16[32,256,256]{1,2,0:T(8,128)(2,1)}), bf16[32,256,256]{1,2,0:T(8,128)(2,1)}, u32[]{:S(2)}, u32[]{:S(2)}) async-start(bf16[32,256,256]{1,2,0:T(8,128)(2,1)} %stack.2), calls=%async_computation | async-start | bytes 8388608 | tf_op jit(solution)/shard_map/all_to_all | solution.py:32
  21.9 204.5 %reduce-scatter.2.cloned.1.call-start = ((), (), s32[]{:S(2)}) async-start(), calls=%async_computation.4 | async-start | bytes 2621440 | tf_op jit(solution)/shard_map/reduce_scatter | solution.py:82
Sparse Core Ops, SparseCore 0:
  9.5 81.6 all-gather.2
  93.4 58.9 all-gather.4
  194.9 31.4 reduce-scatter.1
